TPU v7x, 128 devices: a whole 4x4x4 slice. The times are simulated.
128 devices in a mesh: section: 32 (over y, x, z_lo), tensor: 4 (over z_hi, core).
Axes of the slice: x: 4, y: 4, z: 4 (z_hi: 2, z_lo: 2; z = z_hi * 2 + z_lo), core: 2. Of those that a mesh axis runs over, the one named last changes fastest.
Arguments:
- weights: bfloat16 [32, 4096, 4096], P('section', 'tensor'), may hold values from -0.09375 to 0.09375
- filters: float32 [32, 32, 128], P('section'), may hold values from -0.5 to 0.5
- down_input: bfloat16 [32, 512, 4096], P('section', 'tensor'), may hold values from -6 to 6
- down_cot: bfloat16 [32, 512, 4096], P('section', 'tensor'), may hold values from -6 to 6
- up_input: bfloat16 [32, 512, 4096], P('section', 'tensor'), may hold values from -6 to 6
- up_cot: bfloat16 [32, 512, 4096], P('section', 'tensor'), may hold values from -6 to 6
Outputs:
- weight_grad: bfloat16 [32, 4096, 4096], P('section', 'tensor')
- filter_grad: float32 [32, 32, 128], P('section')
- down_passed: bfloat16 [32, 512, 4096], P('section', 'tensor')
- up_passed: bfloat16 [32, 512, 4096], P('section', 'tensor')
All inputs are finite; a program needn't handle non-finite values.
Results may differ from a plain program's by a relative error of at most 0.014.
Values may be sent and summed in bfloat16 or wider, within the bound.
A program may use at most 192 MiB of HBM per device.

v0:
```python
import jax
import jax.numpy as jnp
from jax import lax
from jax.sharding import PartitionSpec as P

epsilon = 1e-06


def shifted(x, axis, by):
    devices = lax.axis_size(axis)
    pairs = [(i, i + by) for i in range(devices) if 0 <= i + by < devices]
    return lax.ppermute(x, axis, pairs)


def tap_tables(row_count, taps_total):
    target = jnp.arange(row_count, dtype=jnp.int32)[:, None, None]
    source = jnp.arange(row_count + taps_total - 1, dtype=jnp.int32)[None, :, None]
    lag_index = jnp.arange(taps_total, dtype=jnp.int32)[None, None, :]
    causal_table = (target + taps_total - 1 - source == lag_index).astype(jnp.float32)
    ahead_table = (source - target == lag_index).astype(jnp.float32)
    return (causal_table, ahead_table)


def banded(table, filter_taps, extended, row_count):
    group_count = filter_taps.shape[0]
    band = jnp.einsum("tuk,gk->gtu", table, filter_taps, precision=lax.Precision.HIGHEST)
    grouped = extended.reshape(extended.shape[0], extended.shape[1], group_count, -1)
    mixed_out = jnp.einsum("gtu,umgc->tmgc", band, grouped, precision=lax.Precision.HIGHEST)
    return mixed_out.reshape(row_count, extended.shape[1], extended.shape[2])


def layer_grads(inputs, cotangent, weight_rows, filter_taps, tables):
    causal_table, ahead_table = tables
    row_count = inputs.shape[0]
    group_count = filter_taps.shape[0]
    taps_total = filter_taps.shape[1]
    input_wide = inputs.astype(jnp.float32)
    inverse_rms = lax.rsqrt(jnp.mean(input_wide * input_wide, axis=2, keepdims=True) + epsilon)
    normed = input_wide * inverse_rms
    normed_b = normed.astype(jnp.bfloat16)
    feature_rows = lax.all_to_all(normed_b, "tensor", split_axis=2, concat_axis=0, tiled=True)
    selected = feature_rows
    values = lax.psum_scatter(
        jnp.einsum("tmd,de->tme", selected, weight_rows, preferred_element_type=jnp.float32).astype(
            jnp.bfloat16
        ),
        "tensor",
        scatter_dimension=0,
        tiled=True,
    ).astype(jnp.float32)
    before = shifted(
        values[row_count - (taps_total - 1) :].astype(jnp.bfloat16), "tensor", 1
    ).astype(jnp.float32)
    extended = jnp.concatenate([before, values], axis=0)
    convolved = banded(causal_table, filter_taps, extended, row_count)
    cot_wide = cotangent.astype(jnp.float32)
    grad_mix = cot_wide * normed
    following = shifted(grad_mix[: taps_total - 1], "tensor", -1)
    grad_ext = jnp.concatenate([grad_mix, following], axis=0)
    grad_values = banded(ahead_table, filter_taps, grad_ext, row_count)
    grad_grouped = grad_mix.reshape(row_count, grad_mix.shape[1], group_count, -1)
    ext_grouped = extended.reshape(extended.shape[0], extended.shape[1], group_count, -1)
    pairs = jnp.einsum("tmgc,umgc->gtu", grad_grouped, ext_grouped, precision=lax.Precision.HIGHEST)
    tap_part = jnp.einsum("gtu,tuk->gk", pairs, causal_table, precision=lax.Precision.HIGHEST)
    grad_values_b = grad_values.astype(jnp.bfloat16)
    shard_rows = lax.all_gather(grad_values_b, "tensor", axis=0, tiled=True)
    selected = feature_rows
    weight_sum = jnp.einsum("tmd,tme->de", selected, shard_rows, preferred_element_type=jnp.float32)
    returned_rows = jnp.einsum(
        "tme,de->tmd", shard_rows, weight_rows, preferred_element_type=jnp.float32
    )
    back_tokens = lax.all_to_all(
        returned_rows.astype(jnp.bfloat16), "tensor", split_axis=0, concat_axis=2, tiled=True
    ).astype(returned_rows.dtype)
    grad_total = cot_wide * convolved + back_tokens
    projection_mean = jnp.mean(grad_total * normed, axis=2, keepdims=True)
    grad_in = (cot_wide + inverse_rms * (grad_total - normed * projection_mean)).astype(
        jnp.bfloat16
    )
    return (grad_in, weight_sum, tap_part)


def mirrored(stacked):
    sections = lax.axis_size("section")
    pieces = stacked.reshape(
        stacked.shape[0], stacked.shape[1], sections, stacked.shape[2] // sections
    )
    spread = lax.all_to_all(pieces, "section", split_axis=2, concat_axis=2, tiled=True)
    collected = lax.all_to_all(
        jnp.flip(spread, 2), "section", split_axis=2, concat_axis=2, tiled=True
    )
    return collected.reshape(stacked.shape)


def per_device(weights, filters, down_input, down_cot, up_input, up_cot):
    weight_rows = weights[0]
    filter_taps = filters[0]
    tables = tap_tables(down_input.shape[1], filter_taps.shape[1])
    arriving = mirrored(jnp.stack([up_input[0], up_cot[0]], axis=1))
    up_inputs = arriving[:, 0:1]
    up_cotangent = arriving[:, 1:2]
    down_inputs = down_input[0][:, None]
    down_cotangent = down_cot[0][:, None]
    down_result, down_weight, down_taps = layer_grads(
        down_inputs, down_cotangent, weight_rows, filter_taps, tables
    )
    up_grad, up_weight, up_taps = layer_grads(
        up_inputs, up_cotangent, weight_rows, filter_taps, tables
    )
    down_grad = down_result[:, 0]
    weight_part = down_weight + up_weight
    tap_part = down_taps + up_taps
    taps_total = lax.psum(tap_part, "tensor")
    down_passed = shifted(down_grad, "section", -1)
    up_passed = shifted(mirrored(up_grad)[:, 0], "section", 1)
    return (
        weight_part.astype(jnp.bfloat16)[None],
        taps_total[None],
        down_passed[None],
        up_passed[None],
    )


def solution(mesh):
    in_specs = (
        P("section", "tensor", None),
        P("section", None, None),
        P("section", "tensor", None),
        P("section", "tensor", None),
        P("section", "tensor", None),
        P("section", "tensor", None),
    )
    out_specs = (
        P("section", "tensor", None),
        P("section", None, None),
        P("section", "tensor", None),
        P("section", "tensor", None),
    )
    return jax.shard_map(
        per_device, mesh=mesh, in_specs=in_specs, out_specs=out_specs, check_vma=False
    )
```

profile of v0, /device:TPU:34, one launch (start us, length us, event | category | flops | bytes accessed | tf_op | source)
XLA Modules:
  0.0 633.1 jit_solution(15924524114291938445)
XLA Ops:
  13.4 23.4 %reduce.5 = bf16[4096,128]{1,0:T(8,128)(2,1)} reduce(bf16[4096,1,128]{2,1,0:T(2,128)(2,1)S(1)} %bitcast.223, bf16[]{:T(256)} %broadcast.137), dimensions={1}, to_apply=%bitcast.182.reduce_sub_computation | reduce | bytes 2097154
  39.0 20.1 %all_to_all.68 = bf16[4,2,65536]{2,1,0:T(2,128)(2,1)} all-to-all(bf16[4,2,65536]{2,1,0:T(2,128)(2,1)S(1)} %reshape.472), channel_id=1, replica_groups=mesh['section'=32,'tensor'=4] {'tensor'}, dimensions={0} | all-to-all | bytes 2097152 | tf_op jit(solution)/shard_map/all_to_all | solution.py:41
  64.3 9.8 %fusion.26 = bf16[512,1,4096]{2,0,1:T(8,128)(2,1)} fusion(bf16[512,1024]{1,0:T(8,128)(2,1)S(1)} %bitcast.238, bf16[1,1024,4096]{2,1,0:T(8,128)(2,1)} %param.6), kind=kOutput, calls=%fused_computation.23 | convolution fusion | flops 4297064448 | bytes 13631488 | tf_op jit(solution)/shard_map/tmd,de->tme/dot_general | solution.py:44
  81.4 6.6 %copy.99 = f32[127,1,4096]{2,1,0:T(1,128)} copy(f32[127,1,4096]{0,1,2:T(1,128)S(1)} %slice_multiply_fusion) | data formatting | bytes 4161536 | tf_op jit(solution)/shard_map/slice | solution.py:58
  94.0 8.5 %all-to-all-start.1 = ((bf16[128,2,32,128]{0,3,1,2:T(8,128)(2,1)}), bf16[128,2,32,128]{0,3,1,2:T(8,128)(2,1)S(1)}, u32[]{:S(2)}, u32[]{:S(2)}) async-start(bf16[128,2,32,128]{0,3,1,2:T(8,128)(2,1)} %pad_maximum_fusion.1), calls=%async_computation.1 | async-start | bytes 4194304 | tf_op jit(solution)/shard_map/all_to_all | solution.py:88
  103.0 14.0 %fusion.40 = f32[32,128,255]{1,0,2:T(8,128)} fusion(s32[128,255]{0,1:T(8,128)S(1)} %iota_subtract_fusion.1, f32[1,32,128]{2,1,0:T(8,128)S(1)} %copy-done), kind=kOutput, calls=%fused_computation.42 | convolution fusion | flops 1608499200 | bytes 4324864 | tf_op jit(solution)/shard_map/tuk,gk->gtu/dot_general | solution.py:26
  122.2 5.7 copy.100
  127.9 8.7 %fusion.60 = bf16[32,128,128]{2,1,0:T(8,128)(2,1)} fusion(f32[32,128,255]{2,1,0:T(8,128)} %copy.101, f32[127,1,32,128]{0,3,2,1:T(8,128)} %bitcast.229, f32[128,1,32,128]{0,3,2,1:T(8,128)} %get-tuple-element.16), kind=kOutput, calls=%fused_computation.72 | convolution fusion | flops 1605890048 | bytes 9404416 | tf_op jit(solution)/shard_map/gtu,umgc->tmgc/dot_general | solution.py:28
  138.2 25.2 %all_to_all.69 = bf16[128,2,32,128]{0,3,1,2:T(8,128)(2,1)S(1)} all-to-all(bf16[128,2,32,128]{0,3,1,2:T(8,128)(2,1)} %rev.8), channel_id=1, replica_groups=mesh['section'=32,'tensor'=4] {'section'}, dimensions={2} | all-to-all | bytes 4194304 | tf_op jit(solution)/shard_map/all_to_all | solution.py:89
  165.8 17.0 %copy.134 = bf16[128,1,4096]{0,1,2:T(2,128)(2,1)} copy(bf16[128,1,4096]{0,2,1:T(8,128)(2,1)S(1)} %get-tuple-element.21) | data formatting | bytes 2097152 | tf_op jit(solution)/shard_map/convert_element_type | solution.py:40
  182.8 24.4 %reduce.6 = bf16[4096,128]{1,0:T(8,128)(2,1)} reduce(bf16[4096,1,128]{2,1,0:T(2,128)(2,1)} %bitcast.226, bf16[]{:T(256)} %broadcast.137), dimensions={1}, to_apply=%bitcast.203.reduce_sub_computation | reduce | bytes 2097154
  210.8 67.2 %all_to_all.70 = bf16[4,2,65536]{2,1,0:T(2,128)(2,1)} all-to-all(bf16[4,2,65536]{2,1,0:T(2,128)(2,1)} %reshape.474), channel_id=1, replica_groups=mesh['section'=32,'tensor'=4] {'tensor'}, dimensions={0} | all-to-all | bytes 2097152 | tf_op jit(solution)/shard_map/all_to_all | solution.py:41
  286.9 10.2 %fusion.23 = bf16[512,1,4096]{2,0,1:T(8,128)(2,1)} fusion(bf16[512,1024]{1,0:T(8,128)(2,1)} %bitcast.240, bf16[1,1024,4096]{2,1,0:T(8,128)(2,1)} %param.6), kind=kOutput, calls=%fused_computation.22 | convolution fusion | flops 4297064448 | bytes 13631488 | tf_op jit(solution)/shard_map/tmd,de->tme/dot_general | solution.py:44
  297.2 5.7 copy.107
  304.2 6.6 %collective-permute-done.1 = f32[127,1,4096]{2,1,0:T(1,128)} collective-permute-done((f32[127,1,4096]{2,1,0:T(1,128)}, f32[127,1,4096]{2,1,0:T(1,128)}, u32[]{:S(2)}, u32[]{:S(2)}) %collective-permute-start.1) | collective-permute-done | bytes 2080800 | tf_op jit(solution)/shard_map/ppermute | solution.py:12
  310.7 5.7 copy.108
  327.7 39.9 %collective-permute-start.2 = (bf16[127,1,4096]{2,0,1:T(8,128)(2,1)}, bf16[127,1,4096]{2,0,1:T(8,128)(2,1)}, u32[]{:S(2)}, u32[]{:S(2)}) collective-permute-start(bf16[127,1,4096]{2,0,1:T(8,128)(2,1)} %slice.31), channel_id=1, source_target_pairs={{0,1},{1,2},{2,3},{4,5},{5,6},{6,7},{8,9},{9,10},{10,11},{12,13},{... | collective-permute-start | bytes 3121160 | tf_op jit(solution)/shard_map/ppermute | solution.py:12
  367.5 10.8 %fusion.76 = bf16[512,1,1024]{2,0,1:T(8,128)(2,1)} fusion(bf16[1,1024,4096]{2,1,0:T(8,128)(2,1)} %param.6, bf16[512,1,4096]{0,2,1:T(8,128)(2,1)} %all-gather.3.cloned.1.call-done), kind=kOutput, calls=%fused_computation.77 | convolution fusion | flops 4295491584 | bytes 13631488 | tf_op jit(solution)/shard_map/tme,de->tmd/dot_general | solution.py:69
  389.6 14.0 %fusion.41 = f32[32,128,255]{1,0,2:T(8,128)} fusion(s32[128,255]{0,1:T(8,128)S(1)} %iota_subtract_fusion, f32[1,32,128]{2,1,0:T(8,128)S(1)} %copy-done), kind=kOutput, calls=%fused_computation.43 | convolution fusion | flops 1608499200 | bytes 4324864 | tf_op jit(solution)/shard_map/tuk,gk->gtu/dot_general | solution.py:26
  418.7 6.1 copy.120
  437.9 10.2 %fusion.71 = bf16[512,1,1024]{2,0,1:T(8,128)(2,1)} fusion(bf16[1,1024,4096]{2,1,0:T(8,128)(2,1)} %param.6, bf16[512,1,4096]{0,2,1:T(8,128)(2,1)} %all-gather.5.cloned.1.call-done), kind=kOutput, calls=%fused_computation.76 | convolution fusion | flops 4295491584 | bytes 13631488 | tf_op jit(solution)/shard_map/tme,de->tmd/dot_general | solution.py:69
  459.8 8.6 %fusion.54 = (f32[128]{0:T(128)S(1)}, f32[32,128,128]{2,1,0:T(8,128)}) fusion(f32[128,1,32,128]{0,3,2,1:T(8,128)} %bitcast.221, f32[128,1,32,128]{0,3,2,1:T(8,128)} %bitcast.211, f32[128,1,32,128]{0,3,2,1:T(8,128)} %bitcast.214, f32[128]{0:T(128)S(1)} %add_rsqrt_fusion.1, bf16[255,32,128]{0,2,1:T(8,128)(2,1)} %bitcast.219, f32[32,128,255]{2,1,0:T(8,128)} %copy.118), kind=kOutput, calls=%fused_computation.63 | convolution fusion | flops 1606942592 | bytes 14656512 | tf_op jit(solution)/shard_map/gtu,umgc->tmgc/dot_general | solution.py:28
  468.4 7.4 %all-to-all-done.5 = bf16[4,2,65536]{2,1,0:T(2,128)(2,1)} async-done(((bf16[4,2,65536]{2,1,0:T(2,128)(2,1)}), bf16[4,2,65536]{2,1,0:T(2,128)(2,1)}, u32[]{:S(2)}, u32[]{:S(2)}) %all-to-all-start.5) | async-done | bytes 1048608 | tf_op jit(solution)/shard_map/all_to_all | solution.py:72
  479.8 6.1 copy.124
  500.7 10.9 %all-to-all-start.6 = ((bf16[128,1,32,128]{0,3,1,2:T(8,128)(2,1)}), bf16[128,1,32,128]{0,3,1,2:T(8,128)(2,1)}, u32[]{:S(2)}, u32[]{:S(2)}) async-start(bf16[128,1,32,128]{0,3,1,2:T(8,128)(2,1)} %bitcast.235), calls=%async_computation.8 | async-start | bytes 2097152 | tf_op jit(solution)/shard_map/all_to_all | solution.py:88
  518.0 11.9 %all-to-all-done.6 = bf16[128,1,32,128]{0,3,1,2:T(8,128)(2,1)} async-done(((bf16[128,1,32,128]{0,3,1,2:T(8,128)(2,1)}), bf16[128,1,32,128]{0,3,1,2:T(8,128)(2,1)}, u32[]{:S(2)}, u32[]{:S(2)}) %all-to-all-start.6) | async-done | bytes 1048608 | tf_op jit(solution)/shard_map/all_to_all | solution.py:88
  537.6 10.5 %fusion.35 = f32[1024,4096]{1,0:T(8,128)} fusion(bf16[512,1024]{1,0:T(8,128)(2,1)S(1)} %bitcast.239, bf16[512,1,4096]{0,2,1:T(8,128)(2,1)} %all-gather.3.cloned.1.call-done), kind=kOutput, calls=%fused_computation.32 | convolution fusion | flops 4294967296 | bytes 22020096 | tf_op jit(solution)/shard_map/tmd,tme->de/dot_general | solution.py:68
  557.5 11.2 %fusion.81 = f32[32,128]{1,0:T(8,128)S(1)} fusion(f32[32,128,255]{1,0,2:T(8,128)} %copy.113, s32[128,255]{0,1:T(8,128)S(1)} %iota_subtract_fusion), kind=kOutput, calls=%fused_computation.78 | convolution fusion | flops 1608499200 | bytes 4324864 | tf_op jit(solution)/shard_map/gtu,tuk->gk/dot_general | solution.py:64
  576.8 11.4 %fusion.4 = bf16[1,1024,4096]{2,1,0:T(8,128)(2,1)} fusion(f32[1024,4096]{1,0:T(8,128)} %fusion.35, bf16[512,1024]{1,0:T(8,128)(2,1)S(1)} %bitcast.241, bf16[512,1,4096]{0,2,1:T(8,128)(2,1)} %all-gather.5.cloned.1.call-done), kind=kOutput, calls=%fused_computation.7 | convolution fusion | flops 4303355904 | bytes 30408704 | tf_op jit(solution)/shard_map/tmd,tme->de/dot_general | solution.py:68
  593.7 5.5 copy.116
  599.1 11.2 %fusion.84 = f32[1,32,128]{2,1,0:T(8,128)S(1)} fusion(f32[32,128]{1,0:T(8,128)S(1)} %fusion.81, f32[32,128,255]{1,0,2:T(8,128)} %copy.116, s32[128,255]{0,1:T(8,128)S(1)} %iota_subtract_fusion), kind=kOutput, calls=%fused_computation.81 | convolution fusion | flops 1608503296 | bytes 4341248 | tf_op jit(solution)/shard_map/gtu,tuk->gk/dot_general | solution.py:64
  610.3 13.7 %psum.7 = f32[1,32,128]{2,1,0:T(8,128)} all-reduce(f32[1,32,128]{2,1,0:T(8,128)S(1)} %fusion.84), channel_id=1, replica_groups=mesh['section'=32,'tensor'=4] {'tensor'}, use_global_device_ids=true, to_apply=%region_4.5 | all-reduce | flops 4096 | bytes 32768 | tf_op jit(solution)/shard_map/psum | solution.py:113
  (123 shorter events, 170.7 us)
Async XLA Ops:
  7.2 95.8 %copy-start = (f32[1,32,128]{2,1,0:T(8,128)S(1)}, f32[1,32,128]{2,1,0:T(8,128)}, u32[]{:S(2)}) copy-start(f32[1,32,128]{2,1,0:T(8,128)} %param.7) | copy-start | bytes 49156
  7.2 317.9 %reduce-scatter.3.cloned.1.call-start = ((), (), s32[]{:S(2)}) async-start(), calls=%async_computation.12 | async-start | bytes 5242880 | tf_op jit(solution)/shard_map/reduce_scatter | solution.py:43
  9.5 3.4 copy-start.4
  64.3 9.8 %copy-start.14 = (bf16[4,128,1,1024]{3,1,0,2:T(8,128)(2,1)}, bf16[4,128,1,1024]{3,1,0,2:T(8,128)(2,1)S(1)}, u32[]{:S(2)}) copy-start(bf16[4,128,1,1024]{3,1,0,2:T(8,128)(2,1)S(1)} %copy.97) | copy-start | bytes 3145732
  74.1 1.2 copy-start.13
  76.0 1.8 copy-start.9
  76.0 3.1 copy-start.10
  77.8 1.3 copy-start.3
  88.0 34.2 %collective-permute-start = (f32[127,1,4096]{2,1,0:T(1,128)}, f32[127,1,4096]{2,1,0:T(1,128)}, u32[]{:S(2)}, u32[]{:S(2)}) collective-permute-start(f32[127,1,4096]{2,1,0:T(1,128)} %copy.99), channel_id=1, source_target_pairs={{1,0},{2,1},{3,2},{5,4},{6,5},{7,6},{9,8},{10,9},{11,10},{13,12},{... | collective-permute-start | bytes 6242312 | tf_op jit(solution)/shard_map/ppermute | solution.py:12
  94.0 42.7 %all-to-all-start.1 = ((bf16[128,2,32,128]{0,3,1,2:T(8,128)(2,1)}), bf16[128,2,32,128]{0,3,1,2:T(8,128)(2,1)S(1)}, u32[]{:S(2)}, u32[]{:S(2)}) async-start(bf16[128,2,32,128]{0,3,1,2:T(8,128)(2,1)} %pad_maximum_fusion.1), calls=%async_computation.1 | async-start | bytes 4194304 | tf_op jit(solution)/shard_map/all_to_all | solution.py:88
  102.5 265.0 %all-gather.3.cloned.1.call-start = ((), (), s32[]{:S(2)}) async-start(), calls=%async_computation.10 | async-start | bytes 5242880 | tf_op jit(solution)/shard_map/all_gather | solution.py:66
  136.6 295.4 %reduce-scatter.5.cloned.1.call-start = ((), (), s32[]{:S(2)}) async-start(), calls=%async_computation.13 | async-start | bytes 5242880 | tf_op jit(solution)/shard_map/reduce_scatter | solution.py:43
  297.1 140.7 %all-gather.5.cloned.1.call-start = ((), (), s32[]{:S(2)}) async-start(), calls=%async_computation.11 | async-start | bytes 5242880 | tf_op jit(solution)/shard_map/all_gather | solution.py:66
  302.9 7.9 %collective-permute-start.1 = (f32[127,1,4096]{2,1,0:T(1,128)}, f32[127,1,4096]{2,1,0:T(1,128)}, u32[]{:S(2)}, u32[]{:S(2)}) collective-permute-start(f32[127,1,4096]{2,1,0:T(1,128)} %copy.107), channel_id=1, source_target_pairs={{1,0},{2,1},{3,2},{5,4},{6,5},{7,6},{9,8},{10,9},{11,10},{13,12},{... | collective-permute-start | bytes 6242312 | tf_op jit(solution)/shard_map/ppermute | solution.py:12
  316.4 3.4 copy-start.2
  327.7 97.1 %collective-permute-start.2 = (bf16[127,1,4096]{2,0,1:T(8,128)(2,1)}, bf16[127,1,4096]{2,0,1:T(8,128)(2,1)}, u32[]{:S(2)}, u32[]{:S(2)}) collective-permute-start(bf16[127,1,4096]{2,0,1:T(8,128)(2,1)} %slice.31), channel_id=1, source_target_pairs={{0,1},{1,2},{2,3},{4,5},{5,6},{6,7},{8,9},{9,10},{10,11},{12,13},{... | collective-permute-start | bytes 3121160 | tf_op jit(solution)/shard_map/ppermute | solution.py:12
  385.3 29.3 %all-to-all-start.4 = ((bf16[4,2,65536]{2,1,0:T(2,128)(2,1)}), bf16[4,2,65536]{2,1,0:T(2,128)(2,1)}, u32[]{:S(2)}, u32[]{:S(2)}) async-start(bf16[4,2,65536]{2,1,0:T(2,128)(2,1)} %reshape.476), calls=%async_computation.6 | async-start | bytes 2097152 | tf_op jit(solution)/shard_map/all_to_all | solution.py:72
  434.5 51.4 %collective-permute-start.3 = (bf16[127,1,4096]{2,0,1:T(8,128)(2,1)}, bf16[127,1,4096]{2,0,1:T(8,128)(2,1)}, u32[]{:S(2)}, u32[]{:S(2)}) collective-permute-start(bf16[127,1,4096]{2,0,1:T(8,128)(2,1)} %slice.32), channel_id=1, source_target_pairs={{0,1},{1,2},{2,3},{4,5},{5,6},{6,7},{8,9},{9,10},{10,11},{12,13},{... | collective-permute-start | bytes 3121160 | tf_op jit(solution)/shard_map/ppermute | solution.py:12
  455.1 20.7 %all-to-all-start.5 = ((bf16[4,2,65536]{2,1,0:T(2,128)(2,1)}), bf16[4,2,65536]{2,1,0:T(2,128)(2,1)}, u32[]{:S(2)}, u32[]{:S(2)}) async-start(bf16[4,2,65536]{2,1,0:T(2,128)(2,1)} %reshape.478), calls=%async_computation.7 | async-start | bytes 2097152 | tf_op jit(solution)/shard_map/all_to_all | solution.py:72
  493.1 5.3 copy-start.6
  500.7 10.9 %copy-start.8 = (f32[4,128,1,1024]{1,3,0,2:T(8,128)S(1)}, f32[4,128,1,1024]{1,3,0,2:T(8,128)}, u32[]{:S(2)}) copy-start(f32[4,128,1,1024]{1,3,0,2:T(8,128)} %copy.120) | copy-start | bytes 6291460
  500.7 29.2 %all-to-all-start.6 = ((bf16[128,1,32,128]{0,3,1,2:T(8,128)(2,1)}), bf16[128,1,32,128]{0,3,1,2:T(8,128)(2,1)}, u32[]{:S(2)}, u32[]{:S(2)}) async-start(bf16[128,1,32,128]{0,3,1,2:T(8,128)(2,1)} %bitcast.235), calls=%async_computation.8 | async-start | bytes 2097152 | tf_op jit(solution)/shard_map/all_to_all | solution.py:88
  515.4 22.2 %copy-start.15 = (bf16[4,128,1,1024]{3,1,0,2:T(8,128)(2,1)S(1)}, bf16[4,128,1,1024]{3,1,0,2:T(8,128)(2,1)}, u32[]{:S(2)}) copy-start(bf16[4,128,1,1024]{3,1,0,2:T(8,128)(2,1)} %copy-done.14) | copy-start | bytes 3145732
  515.4 53.3 %collective-permute-start.4 = (bf16[128,4096]{0,1:T(8,128)(2,1)}, bf16[128,4096]{0,1:T(8,128)(2,1)S(1)}, u32[]{:S(2)}, u32[]{:S(2)}) collective-permute-start(bf16[128,4096]{0,1:T(8,128)(2,1)} %fusion.51), channel_id=1, source_target_pairs={{4,0},{8,4},{12,8},{16,12},{20,16},{24,20},{28,24},{32,28},{36,32}... | collective-permute-start | bytes 3145736 | tf_op jit(solution)/shard_map/ppermute | solution.py:12
  532.2 39.8 %all-to-all-start.7 = ((bf16[128,1,32,128]{0,3,1,2:T(8,128)(2,1)}), bf16[128,1,32,128]{0,3,1,2:T(8,128)(2,1)S(1)}, u32[]{:S(2)}, u32[]{:S(2)}) async-start(bf16[128,1,32,128]{0,3,1,2:T(8,128)(2,1)} %rev.9), calls=%async_computation.9 | async-start | bytes 2097152 | tf_op jit(solution)/shard_map/all_to_all | solution.py:89
  537.6 10.5 %copy-start.7 = (bf16[255,1,4096]{0,2,1:T(8,128)(2,1)S(1)}, bf16[255,1,4096]{0,2,1:T(8,128)(2,1)}, u32[]{:S(2)}) copy-start(bf16[255,1,4096]{0,2,1:T(8,128)(2,1)} %copy.131) | copy-start | bytes 6266884
  537.6 10.5 %copy-start.11 = (f32[128,32,128]{2,0,1:T(8,128)S(1)}, f32[128,32,128]{2,0,1:T(8,128)}, u32[]{:S(2)}) copy-start(f32[128,32,128]{2,0,1:T(8,128)} %copy.111) | copy-start | bytes 6291460
  537.6 10.5 %copy-start.12 = (f32[128,32,128]{2,0,1:T(8,128)S(1)}, f32[128,32,128]{2,0,1:T(8,128)}, u32[]{:S(2)}) copy-start(f32[128,32,128]{2,0,1:T(8,128)} %copy.110) | copy-start | bytes 6291460
  569.6 7.2 %copy-start.16 = (bf16[4,128,1,1024]{3,1,0,2:T(8,128)(2,1)S(1)}, bf16[4,128,1,1024]{3,1,0,2:T(8,128)(2,1)}, u32[]{:S(2)}) copy-start(bf16[4,128,1,1024]{3,1,0,2:T(8,128)(2,1)} %copy.106) | copy-start | bytes 3145732
  573.3 15.0 %copy-start.5 = (f32[128,1,4096]{0,2,1:T(8,128)S(1)}, f32[128,1,4096]{0,2,1:T(8,128)}, u32[]{:S(2)}) copy-start(f32[128,1,4096]{0,2,1:T(8,128)} %get-tuple-element.20) | copy-start | bytes 6291460
  573.3 50.7 %collective-permute-start.5 = (bf16[128,4096]{1,0:T(8,128)(2,1)}, bf16[128,4096]{1,0:T(8,128)(2,1)}, u32[]{:S(2)}, u32[]{:S(2)}) collective-permute-start(bf16[128,4096]{1,0:T(8,128)(2,1)} %copy.126), channel_id=1, source_target_pairs={{0,4},{4,8},{8,12},{12,16},{16,20},{20,24},{24,28},{28,32},{32,36}... | collective-permute-start | bytes 3145736 | tf_op jit(solution)/shard_map/ppermute | solution.py:12
  599.1 27.2 %copy-start.1 = (f32[1,32,128]{2,1,0:T(8,128)S(1)}, f32[1,32,128]{2,1,0:T(8,128)}, u32[]{:S(2)}) copy-start(f32[1,32,128]{2,1,0:T(8,128)} %param.7) | copy-start | bytes 49156
  (1 other events, 1.0 us)
Sparse Core Ops, SparseCore 0:
  74.3 94.8 reduce-scatter.2
  171.5 62.1 all-gather.2
  297.3 57.9 reduce-scatter.4
  356.8 53.8 all-gather.4
where the time goes:
time: 646 us; the launch traced here: 633 us
  matrix products  150 us (23%)
  local copies, waits for them, and re-layouts  149 us (23%)
  blocking collectives  126 us (20%)
  starting transfers between devices  86 us (13%)
  other arithmetic  81.3 us (13%)
  waiting for transfers between devices  26 us (4%)
  between operations  14.4 us (2%)
    all_to_all x2, blocking collectives, layer_grads(): lax.all_to_all(normed_b, 'tensor', split_axis=2, concat_axis=0, tiled=True)  87.3 us
    ppermute x6, starting transfers between devices, shifted(): return lax.ppermute(x, axis, pairs)  51.8 us
    unnamed x2, other arithmetic  47.8 us
    unnamed x53, local copies, waits for them, and re-layouts  46.5 us
    dot_general x2, matrix products, banded(): jnp.einsum('tuk,gk->gtu', table, filter_taps, precision=lax.Precision.HIG...  28 us
    dot_general x4, matrix products, banded(): jnp.einsum('gtu,umgc->tmgc', band, grouped, precision=lax.Precision.HIGHEST)  27.9 us
    all_to_all x1, blocking collectives, mirrored(): lax.all_to_all(jnp.flip(spread, 2), 'section', split_axis=2, concat_axis=...  25.2 us
    dot_general x2, matrix products, layer_grads(): jnp.einsum('gtu,tuk->gk', pairs, causal_table, precision=lax.Precision.HI...  22.3 us
  transfers between devices with their start and end apart: 15, of which 3 were waited for; matrix products, arithmetic and copies ran while one was open for 49% of the time, Pallas kernels for 0%

commit v1 on v0

v1 whole, which is shorter than its diff:
```python
import functools

import jax
import jax.numpy as jnp
from jax import lax
from jax.experimental import pallas as pl
from jax.experimental.pallas import tpu as pltpu
from jax.sharding import PartitionSpec as P

epsilon = 1e-06
MESH = pl.DeviceIdType.MESH
bf16 = jnp.bfloat16
f32 = jnp.float32
NT = 4


def contract_last(a, b):
    return lax.dot_general(a, b, (((1,), (1,)), ((), ())), preferred_element_type=f32)


def matmul(a, b):
    return jnp.dot(a, b, preferred_element_type=f32)


def kernel(
    sections,
    w_hbm, f_ref, xd_hbm, cd_hbm, xu_hbm, cu_hbm,
    dw_hbm, fg_hbm, od_hbm, ou_hbm,
    W, X, C, R, OWN, U, RS, T, TC, NBT, GV, VS, V, VR, G, PM, OS, FG, DW,
    g_send, g_recv, r_send, r_recv, u_send, u_recv, v_send, v_recv,
    gv_send, gv_recv, pm_send, pm_recv, o_send, o_recv, fg_send, fg_recv,
    w_sem, own_sem, dw_sem,
):
    S = sections
    s = lax.axis_index("section")
    t = lax.axis_index("tensor")
    h = t // 2
    c = t % 2
    sib = (s, h * 2 + (1 - c))
    TB, D = xd_hbm.shape
    BW = D // NT
    CW = 2 * BW
    TOK = NT * TB
    groups = f_ref.shape[0]
    per_block = groups // NT
    n_groups = 2 * per_block
    gw = D // groups
    flip = s + 1 - 2 * (s % 2)
    mirror = S - 1 - s
    relay = mirror + 1 - 2 * (mirror % 2)
    prev_s = lax.rem(s + S - 1, S)
    next_s = lax.rem(s + 1, S)
    up_s = lax.rem(S - s, S)
    up_self = up_s == s

    barrier = pltpu.get_barrier_semaphore()

    def greet(dev):
        pl.semaphore_signal(barrier, inc=1, device_id=dev, device_id_type=MESH)

    for q in range(1, NT):
        greet((s, lax.rem(t + q, NT)))
    greet((relay, t))
    for q in range(NT):
        greet((flip, q))
        greet((next_s, q))
    for q in range(NT):
        own = jnp.logical_and(up_self, t == q)

        @pl.when(jnp.logical_not(own))
        def _():
            greet((up_s, q))

    w_copy = pltpu.make_async_copy(w_hbm, W, w_sem)
    w_copy.start()
    own_copy = pltpu.make_async_copy(xd_hbm, OWN, own_sem)
    own_copy.start()
    pl.semaphore_wait(barrier, jnp.where(up_self, 15, 16))

    my_rows = pl.ds(pl.multiple_of(t * TB, TB), TB)

    def piece(src, dst_ref, mb, arr, q, i, dev, src_t):
        return pltpu.make_async_remote_copy(
            src_ref=src.at[:, pl.ds((2 * i + q % 2) * BW, BW)],
            dst_ref=dst_ref.at[mb, pl.ds(pl.multiple_of(src_t * TB, TB), TB), pl.ds(i * BW, BW)],
            send_sem=g_send.at[mb, arr, q, i],
            recv_sem=g_recv.at[mb, arr, src_t, i],
            device_id=dev,
            device_id_type=MESH,
        )

    def local_piece(src, dst_ref, mb, arr, q, i):
        return pltpu.make_async_copy(
            src.at[:, pl.ds((2 * i + q % 2) * BW, BW)],
            dst_ref.at[mb, pl.ds(q * TB, TB), pl.ds(i * BW, BW)],
            g_recv.at[mb, arr, q, i],
        )

    for arr, (src, dst) in enumerate(((xd_hbm, X), (cd_hbm, C))):
        for q in range(NT):
            @pl.when(t != q)
            def _():
                for i in range(2):
                    piece(src, dst, 0, arr, q, i, (s, q), t).start()

            @pl.when(t == q)
            def _():
                for i in range(2):
                    local_piece(src, dst, 0, arr, q, i).start()

    def relay_copy(arr):
        return pltpu.make_async_remote_copy(
            src_ref=(xu_hbm, cu_hbm)[arr], dst_ref=U.at[arr],
            send_sem=u_send.at[arr], recv_sem=u_recv.at[arr],
            device_id=(relay, t), device_id_type=MESH,
        )

    for arr in range(2):
        relay_copy(arr).start()

    def inverse_rms(ref):
        def step(j, acc):
            x = ref[:, pl.ds(pl.multiple_of(j * gw, gw), gw)].astype(f32)
            return acc + x * x
        acc = lax.fori_loop(0, D // gw, step, jnp.zeros((TB, gw), f32))
        mean = jnp.sum(acc, axis=1, keepdims=True) / D
        return jnp.broadcast_to(lax.rsqrt(mean + epsilon), (TB, 128))

    def r_copy(mb, q, dev):
        return pltpu.make_async_remote_copy(
            src_ref=RS.at[mb], dst_ref=R.at[mb, my_rows, :],
            send_sem=r_send.at[mb, q], recv_sem=r_recv.at[mb, t],
            device_id=dev, device_id_type=MESH,
        )

    own_copy.wait()
    RS[0] = inverse_rms(OWN)
    for q in range(NT):
        @pl.when(t != q)
        def _():
            r_copy(0, q, (s, q)).start()

        @pl.when(t == q)
        def _():
            R[0, q * TB : (q + 1) * TB, :] = RS[0]

    rows = lax.broadcasted_iota(jnp.int32, (TB, 2 * TB), 0)

    def build(gi, carry):
        g = (gi // per_block * 2 + c) * per_block + lax.rem(gi, per_block)
        taps = jnp.broadcast_to(f_ref[pl.ds(g, 1), :], (TB, TB))
        x = jnp.concatenate([taps, jnp.zeros((TB, TB), f32)], axis=1)
        step = 1
        while step < TB:
            x = jnp.where((rows & step) != 0, pltpu.roll(x, step, 1), x)
            step *= 2
        T[gi] = x.astype(bf16)
        TC[gi] = jnp.concatenate([x[:, TB:].T, x[:, :TB].T], axis=1).astype(bf16)
        return carry

    lax.fori_loop(0, n_groups, build, 0)
    FG[...] = jnp.zeros_like(FG)

    def gather_wait(mb):
        for arr, dst in enumerate((X, C)):
            for q in range(NT):
                for i in range(2):
                    pltpu.make_async_copy(
                        dst.at[mb, pl.ds(q * TB, TB), pl.ds(i * BW, BW)],
                        dst.at[mb, pl.ds(q * TB, TB), pl.ds(i * BW, BW)],
                        g_recv.at[mb, arr, q, i],
                    ).wait()
        for q in range(NT):
            def wait_r():
                pltpu.make_async_copy(RS.at[mb], R.at[mb, pl.ds(q * TB, TB), :], r_recv.at[mb, q]).wait()
            if mb == 0:
                pl.when(t != q)(wait_r)
            else:
                wait_r()

    gather_wait(0)

    for arr in range(2):
        relay_copy(arr).wait_recv()
        for q in range(NT):
            for i in range(2):
                piece(U.at[arr], (X, C)[arr], 1, arr, q, i, (flip, q), t).start()
    RS[1] = inverse_rms(U.at[0])
    for q in range(NT):
        r_copy(1, q, (flip, q)).start()

    def cols(j, width=gw):
        return pl.ds(pl.multiple_of(j * width, width), width)

    def natural(gi):
        return (gi // per_block * 2 + c) * per_block + lax.rem(gi, per_block)

    def windows(x):
        return jnp.concatenate([x[i * TB : (i + 2) * TB] for i in range(NT)], axis=1)

    zero_block = jnp.zeros((TB, gw), bf16)

    def gv_copy(mb, i):
        blk = pl.ds(pl.multiple_of((2 * i + c) * BW, BW), BW)
        return pltpu.make_async_remote_copy(
            src_ref=GV.at[pl.ds(mb * TOK, TOK), blk], dst_ref=GV.at[pl.ds(mb * TOK, TOK), blk],
            send_sem=gv_send.at[mb, i], recv_sem=gv_recv.at[mb, i],
            device_id=sib, device_id_type=MESH,
        )

    def v_copy(mb):
        return pltpu.make_async_remote_copy(
            src_ref=VS, dst_ref=VR.at[mb],
            send_sem=v_send.at[mb], recv_sem=v_recv.at[mb],
            device_id=sib, device_id_type=MESH,
        )

    def pm_copy(mb):
        return pltpu.make_async_remote_copy(
            src_ref=PM.at[mb, 0], dst_ref=PM.at[mb, 1],
            send_sem=pm_send.at[mb], recv_sem=pm_recv.at[mb],
            device_id=sib, device_id_type=MESH,
        )

    VN = min(512, BW)
    RN = min(256, BW)

    def layer(mb):
        def prep(gi, carry):
            n = X[mb, :, cols(gi)].astype(f32) * R[mb]
            gm = (C[mb, :, cols(gi)].astype(f32) * n).astype(bf16)
            X[mb, :, cols(gi)] = n.astype(bf16)
            w = windows(jnp.concatenate([gm, zero_block], axis=0))
            gv = matmul(T[gi], w).astype(bf16)
            for i in range(NT):
                GV[mb * TOK + i * TB : mb * TOK + (i + 1) * TB, cols(natural(gi))] = gv[:, i * gw : (i + 1) * gw]
            return carry

        lax.fori_loop(0, n_groups, prep, 0)
        for i in range(2):
            gv_copy(mb, i).start()

        own_cols = pl.ds(pl.multiple_of(h * BW, BW), BW)

        def sib_values(j, carry):
            src = (j // (BW // VN) * 2 + (1 - c)) * (BW // VN) + lax.rem(j, BW // VN)
            VS[:, cols(j, VN)] = matmul(X[mb, :, own_cols], W[:, cols(src, VN)]).astype(bf16)
            return carry

        def own_values(j, carry):
            src = (j // (BW // VN) * 2 + c) * (BW // VN) + lax.rem(j, BW // VN)
            V[:, cols(j, VN)] = matmul(X[mb, :, own_cols], W[:, cols(src, VN)]).astype(bf16)
            return carry

        lax.fori_loop(0, CW // VN, sib_values, 0)
        v_copy(mb).start()
        lax.fori_loop(0, CW // VN, own_values, 0)

        def turn(j, carry):
            n = X[mb, :, cols(h * per_block + j)].astype(f32)
            NBT[cols(j), mb * TOK : (mb + 1) * TOK] = n.T.astype(bf16)
            return carry

        lax.fori_loop(0, per_block, turn, 0)
        v_copy(mb).wait_recv()

        def mix(gi, carry):
            v = (V[:, cols(gi)].astype(f32) + VR[mb, :, cols(gi)].astype(f32)).astype(bf16)
            cot = C[mb, :, cols(gi)].astype(f32)
            gm = (cot * X[mb, :, cols(gi)].astype(f32)).astype(bf16)
            conv = matmul(TC[gi], windows(jnp.concatenate([zero_block, v], axis=0)))
            for i in range(NT):
                part = slice(i * TB, (i + 1) * TB)
                G[part, cols(gi)] = (cot[part] * conv[:, i * gw : (i + 1) * gw]).astype(bf16)
            v_side = jnp.concatenate([v[i * TB : (i + 1) * TB] for i in range(NT)], axis=1)
            x = contract_last(v_side, windows(jnp.concatenate([gm, zero_block], axis=0)))
            n = TB
            while n > 1:
                half = n // 2
                x = x[:half] + pltpu.roll(x[half:n], 2 * TB - half, 1)
                n = half
            FG[pl.ds(gi, 1), :] = FG[pl.ds(gi, 1), :] + x[:, :TB]
            return carry

        lax.fori_loop(0, n_groups, mix, 0)

        for i in range(2):
            blk = pl.ds(pl.multiple_of((2 * i + 1 - c) * BW, BW), BW)
            pltpu.make_async_copy(
                GV.at[pl.ds(mb * TOK, TOK), blk], GV.at[pl.ds(mb * TOK, TOK), blk], gv_recv.at[mb, i]
            ).wait()

        def returned(j, carry):
            res = contract_last(GV[mb * TOK : (mb + 1) * TOK, :], W[pl.ds(pl.multiple_of(j * RN, RN), RN), :])
            at = cols(h * (BW // RN) + j, RN)
            G[:, at] = (G[:, at].astype(f32) + res).astype(bf16)
            return carry

        lax.fori_loop(0, BW // RN, returned, 0)

        def moment(gi, acc):
            return acc + G[:, cols(gi)].astype(f32) * X[mb, :, cols(gi)].astype(f32)

        PM[mb, 0] = lax.fori_loop(0, n_groups, moment, jnp.zeros((TOK, gw), f32))
        pm_copy(mb).start()
        pm_copy(mb).wait_recv()
        mean = jnp.sum(PM[mb, 0] + PM[mb, 1], axis=1, keepdims=True) / D
        PM[mb, 1] = jnp.broadcast_to(mean, (TOK, gw))
        keep = jnp.where(h == 0, 1.0, 0.0).astype(f32)

        def final(gi, carry):
            n = X[mb, :, cols(gi)].astype(f32)
            grad = R[mb] * (G[:, cols(gi)].astype(f32) - n * PM[mb, 1])
            OS[mb, :, cols(gi)] = (grad + keep * C[mb, :, cols(gi)].astype(f32)).astype(bf16)
            return carry

        lax.fori_loop(0, n_groups, final, 0)

    def out_blk(i):
        return pl.ds(pl.multiple_of((2 * i + c) * BW, BW), BW)

    def out_remote(mb, q, i):
        dst, sec = ((od_hbm, prev_s), (ou_hbm, up_s))[mb]
        return pltpu.make_async_remote_copy(
            src_ref=OS.at[mb, pl.ds(q * TB, TB), pl.ds(i * BW, BW)],
            dst_ref=dst.at[h, :, out_blk(i)],
            send_sem=o_send.at[mb, q, i], recv_sem=o_recv.at[mb, t, i],
            device_id=(sec, q), device_id_type=MESH,
        )

    def out_local(q, i):
        return pltpu.make_async_copy(
            OS.at[1, pl.ds(q * TB, TB), pl.ds(i * BW, BW)], ou_hbm.at[h, :, out_blk(i)], o_recv.at[1, q, i]
        )

    w_copy.wait()
    layer(0)
    v_copy(0).wait_send()
    gather_wait(1)
    for q in range(NT):
        for i in range(2):
            out_remote(0, q, i).start()
    layer(1)
    for q in range(NT):
        own = jnp.logical_and(up_self, t == q)
        for i in range(2):
            @pl.when(own)
            def _():
                out_local(q, i).start()

            @pl.when(jnp.logical_not(own))
            def _():
                out_remote(1, q, i).start()

    def fg_copy(q):
        return pltpu.make_async_remote_copy(
            src_ref=FG, dst_ref=fg_hbm.at[t], send_sem=fg_send.at[q], recv_sem=fg_recv.at[t],
            device_id=(s, q), device_id_type=MESH,
        )

    for q in range(NT):
        @pl.when(t != q)
        def _():
            fg_copy(q).start()

        @pl.when(t == q)
        def _():
            pltpu.make_async_copy(FG, fg_hbm.at[q], fg_recv.at[q]).start()

    DN = min(512, BW)
    tiles = D // DN

    def dw_copy(j, slot):
        return pltpu.make_async_copy(DW.at[slot], dw_hbm.at[:, cols(j, DN)], dw_sem.at[slot])

    def dw_tile(j, carry):
        slot = lax.rem(j, 2)

        @pl.when(j >= 2)
        def _():
            dw_copy(j - 2, slot).wait()

        DW[slot] = matmul(NBT[...], GV[:, cols(j, DN)]).astype(bf16)
        dw_copy(j, slot).start()
        return carry

    lax.fori_loop(0, tiles, dw_tile, 0)
    for j in (tiles - 2, tiles - 1):
        dw_copy(j, j % 2).wait()

    for arr in range(2):
        relay_copy(arr).wait_send()
    for q in range(NT):
        @pl.when(t != q)
        def _():
            for arr, (src, dst) in enumerate(((xd_hbm, X), (cd_hbm, C))):
                for i in range(2):
                    piece(src, dst, 0, arr, q, i, (s, q), t).wait_send()
            r_copy(0, q, (s, q)).wait_send()
            fg_copy(q).wait_send()

        for arr in range(2):
            for i in range(2):
                piece(U.at[arr], (X, C)[arr], 1, arr, q, i, (flip, q), t).wait_send()
        r_copy(1, q, (flip, q)).wait_send()
        pltpu.make_async_copy(FG, fg_hbm.at[q], fg_recv.at[q]).wait()
        own = jnp.logical_and(up_self, t == q)
        for i in range(2):
            out_remote(0, q, i).wait_send()

            @pl.when(jnp.logical_not(own))
            def _():
                out_remote(1, q, i).wait_send()
    v_copy(1).wait_send()
    for mb in range(2):
        pm_copy(mb).wait_send()
        for i in range(2):
            gv_copy(mb, i).wait_send()
    for mb, dst in enumerate((od_hbm, ou_hbm)):
        for q in range(NT):
            for i in range(2):
                landed = dst.at[q // 2, :, pl.ds((2 * i + q % 2) * BW, BW)]
                pltpu.make_async_copy(landed, landed, o_recv.at[mb, q, i]).wait()


def per_device(sections, weights, filters, down_input, down_cot, up_input, up_cot):
    w = weights[0]
    taps = filters[0]
    BW, D = w.shape
    TB = down_input.shape[1]
    CW = 2 * BW
    TOK = NT * TB
    groups, K = taps.shape
    n_groups = groups // 2
    hbm = pl.BlockSpec(memory_space=pl.ANY)
    dma = pltpu.SemaphoreType.DMA
    DN = min(512, BW)
    dw, fg, od, ou = pl.pallas_call(
        functools.partial(kernel, sections),
        out_shape=(
            jax.ShapeDtypeStruct((BW, D), bf16),
            jax.ShapeDtypeStruct((NT, n_groups, K), f32),
            jax.ShapeDtypeStruct((2, TB, D), bf16),
            jax.ShapeDtypeStruct((2, TB, D), bf16),
        ),
        in_specs=[hbm, pl.BlockSpec(memory_space=pltpu.VMEM), hbm, hbm, hbm, hbm],
        out_specs=(hbm, hbm, hbm, hbm),
        scratch_shapes=[
            pltpu.VMEM((BW, D), bf16),
            pltpu.VMEM((2, TOK, CW), bf16),
            pltpu.VMEM((2, TOK, CW), bf16),
            pltpu.VMEM((2, TOK, 128), f32),
            pltpu.VMEM((TB, D), bf16),
            pltpu.VMEM((2, TB, D), bf16),
            pltpu.VMEM((2, TB, 128), f32),
            pltpu.VMEM((n_groups, TB, 2 * TB), bf16),
            pltpu.VMEM((n_groups, TB, 2 * TB), bf16),
            pltpu.VMEM((BW, 2 * TOK), bf16),
            pltpu.VMEM((2 * TOK, D), bf16),
            pltpu.VMEM((TOK, CW), bf16),
            pltpu.VMEM((TOK, CW), bf16),
            pltpu.VMEM((2, TOK, CW), bf16),
            pltpu.VMEM((TOK, CW), bf16),
            pltpu.VMEM((2, 2, TOK, 128), f32),
            pltpu.VMEM((2, TOK, CW), bf16),
            pltpu.VMEM((n_groups, K), f32),
            pltpu.VMEM((2, BW, DN), bf16),
            dma((2, 2, NT, 2)), dma((2, 2, NT, 2)), dma((2, NT)), dma((2, NT)),
            dma((2,)), dma((2,)), dma((2,)), dma((2,)),
            dma((2, 2)), dma((2, 2)), dma((2,)), dma((2,)),
            dma((2, NT, 2)), dma((2, NT, 2)), dma((NT,)), dma((NT,)),
            dma, dma, dma((2,)),
        ],
        compiler_params=pltpu.CompilerParams(
            collective_id=0, has_side_effects=True, vmem_limit_bytes=60 * 1024 * 1024
        ),
        name="relay_backward",
    )(w, taps, down_input[0], down_cot[0], up_input[0], up_cot[0])
    s = lax.axis_index("section")
    down = od[0].astype(f32) + od[1].astype(f32)
    up = ou[0].astype(f32) + ou[1].astype(f32)
    down = jnp.where(s == sections - 1, 0.0, down).astype(bf16)
    up = jnp.where(s == 0, 0.0, up).astype(bf16)
    fg = fg.reshape(2, 2, 2, groups // NT, K)
    fg = jnp.transpose(fg[0] + fg[1], (1, 0, 2, 3)).reshape(groups, K)
    return dw[None], fg[None], down[None], up[None]


def solution(mesh):
    row = P("section", "tensor", None)
    whole = P("section", None, None)
    return jax.shard_map(
        functools.partial(per_device, mesh.shape["section"]),
        mesh=mesh,
        in_specs=(row, whole, row, row, row, row),
        out_specs=(row, whole, row, row),
        check_vma=False,
    )
```

time: 646 us -> 224 us (0.35)
  the two profiles are of different devices: /device:TPU:34 before, /device:TPU:91 now
where the time goes in v1:
time: 224 us
  Pallas kernels  211 us (94%)
  local copies, waits for them, and re-layouts  8.5 us (4%)
  other arithmetic  4.27 us (2%)
    pallas_call x1, Pallas kernels, per_device(): pl.pallas_call(functools.partial(kernel, sections), out_shape=(jax.ShapeD...  211 us
    unnamed x3, local copies, waits for them, and re-layouts  7.89 us

profile of v1, /device:TPU:91, one launch (start us, length us, event | category | flops | bytes accessed | tf_op | source)
XLA Modules:
  0.0 224.2 jit_solution(140370578580152254)
XLA Ops:
  0.6 210.8 %relay_backward.1 = (bf16[1024,4096]{1,0:T(8,128)(2,1)}, f32[4,16,128]{2,1,0:T(8,128)}, bf16[2,128,4096]{2,1,0:T(8,128)(2,1)}, bf16[2,128,4096]{2,1,0:T(8,128)(2,1)}) custom-call(bf16[1024,4096]{1,0:T(8,128)(2,1)} %bitcast.12, f32[32,128]{1,0:T(8,128)} %bitcast.18, bf16[128,4096]{1,0:T(8,128)(2,1)} %bitcast.14, bf16[128,4096]{1,0:T(8,128)(2,1)} %bitcast.15, ...), custom_call_target="tpu_custom_call" | custom-call | tf_op jit(solution)/shard_map/relay_backward/pallas_call | solution.py:438
  211.4 0.0 copy-start
  211.5 4.3 %select_convert_fusion = (bf16[1,128,4096]{2,1,0:T(8,128)(2,1)}, bf16[1,128,4096]{2,1,0:T(8,128)(2,1)}) fusion(bf16[2,128,4096]{2,1,0:T(8,128)(2,1)} %get-tuple-element.11, pred[]{:T(512)S(6)} %eq.7, bf16[2,128,4096]{2,1,0:T(8,128)(2,1)} %get-tuple-element.10, pred[]{:T(512)S(6)} %eq.6), kind=kLoop, calls=%fused_computation | loop fusion | flops 5242880 | bytes 6291458 | tf_op jit(solution)/shard_map/convert_element_type | solution.py:483
  215.7 0.0 copy-done
  215.7 0.6 copy.10
  216.3 7.9 %copy.12 = bf16[1,1024,4096]{2,1,0:T(8,128)(2,1)} copy(bf16[1,1024,4096]{2,1,0:T(8,128)(2,1)} %bitcast.13) | data formatting | bytes 16777216
  (1 shorter events, 0.0 us)
Async XLA Ops:
  211.4 4.3 %copy-start = (f32[4,16,128]{2,1,0:T(8,128)S(1)}, f32[4,16,128]{2,1,0:T(8,128)}, u32[]{:S(2)}) copy-start(f32[4,16,128]{2,1,0:T(8,128)} %get-tuple-element.9) | copy-start | bytes 98308

commit v2 on v1

--- a/solution.py
+++ b/solution.py
@@ -26,9 +26,9 @@
     sections,
     w_hbm, f_ref, xd_hbm, cd_hbm, xu_hbm, cu_hbm,
     dw_hbm, fg_hbm, od_hbm, ou_hbm,
-    W, X, C, R, OWN, U, RS, T, TC, NBT, GV, VS, V, VR, G, PM, OS, FG, DW,
+    W, X, C, R, OWN, U, RS, T, TC, NBT, GV, VS, V, VR, G, PM, OS, RB, FG, DW,
     g_send, g_recv, r_send, r_recv, u_send, u_recv, v_send, v_recv,
-    gv_send, gv_recv, pm_send, pm_recv, o_send, o_recv, fg_send, fg_recv,
+    gv_send, gv_recv, pm_send, pm_recv, o_send, o_recv, f_send, f_recv, fg_send, fg_recv,
     w_sem, own_sem, dw_sem,
 ):
     S = sections
@@ -48,8 +48,8 @@
     flip = s + 1 - 2 * (s % 2)
     mirror = S - 1 - s
     relay = mirror + 1 - 2 * (mirror % 2)
-    prev_s = lax.rem(s + S - 1, S)
-    next_s = lax.rem(s + 1, S)
+    odd = s % 2 == 1
+    down_s = lax.rem(s + S - 2, S)
     up_s = lax.rem(S - s, S)
     up_self = up_s == s
 
@@ -63,19 +63,20 @@
     greet((relay, t))
     for q in range(NT):
         greet((flip, q))
-        greet((next_s, q))
-    for q in range(NT):
-        own = jnp.logical_and(up_self, t == q)
-
-        @pl.when(jnp.logical_not(own))
-        def _():
-            greet((up_s, q))
+
+    @pl.when(odd)
+    def _():
+        greet((lax.rem(s + 2, S), t))
+
+    @pl.when(jnp.logical_not(up_self))
+    def _():
+        greet((up_s, t))
 
     w_copy = pltpu.make_async_copy(w_hbm, W, w_sem)
     w_copy.start()
     own_copy = pltpu.make_async_copy(xd_hbm, OWN, own_sem)
     own_copy.start()
-    pl.semaphore_wait(barrier, jnp.where(up_self, 15, 16))
+    pl.semaphore_wait(barrier, 8 + jnp.where(odd, 1, 0) + jnp.where(up_self, 0, 1))
 
     my_rows = pl.ds(pl.multiple_of(t * TB, TB), TB)
 
@@ -225,7 +226,7 @@
     VN = min(512, BW)
     RN = min(256, BW)
 
-    def layer(mb):
+    def layer(mb, between):
         def prep(gi, carry):
             n = X[mb, :, cols(gi)].astype(f32) * R[mb]
             gm = (C[mb, :, cols(gi)].astype(f32) * n).astype(bf16)
@@ -284,6 +285,8 @@
 
         lax.fori_loop(0, n_groups, mix, 0)
 
+        if between is not None:
+            between(0, 0)
         for i in range(2):
             blk = pl.ds(pl.multiple_of((2 * i + 1 - c) * BW, BW), BW)
             pltpu.make_async_copy(
@@ -297,6 +300,8 @@
             return carry
 
         lax.fori_loop(0, BW // RN, returned, 0)
+        if between is not None:
+            between(0, 1)
 
         def moment(gi, acc):
             return acc + G[:, cols(gi)].astype(f32) * X[mb, :, cols(gi)].astype(f32)
@@ -316,41 +321,97 @@
 
         lax.fori_loop(0, n_groups, final, 0)
 
-    def out_blk(i):
-        return pl.ds(pl.multiple_of((2 * i + c) * BW, BW), BW)
-
-    def out_remote(mb, q, i):
-        dst, sec = ((od_hbm, prev_s), (ou_hbm, up_s))[mb]
-        return pltpu.make_async_remote_copy(
-            src_ref=OS.at[mb, pl.ds(q * TB, TB), pl.ds(i * BW, BW)],
-            dst_ref=dst.at[h, :, out_blk(i)],
-            send_sem=o_send.at[mb, q, i], recv_sem=o_recv.at[mb, t, i],
-            device_id=(sec, q), device_id_type=MESH,
-        )
-
-    def out_local(q, i):
-        return pltpu.make_async_copy(
-            OS.at[1, pl.ds(q * TB, TB), pl.ds(i * BW, BW)], ou_hbm.at[h, :, out_blk(i)], o_recv.at[1, q, i]
-        )
+    HB = TB // 2
+    CHUNKS = 4
+
+    def out_src(mb, q, k):
+        return OS.at[mb, pl.ds(q * TB + k % 2 * HB, HB), pl.ds(k // 2 * BW, BW)]
+
+    def out_dst(mb, k):
+        blk = pl.ds(pl.multiple_of((k // 2 * 2 + c) * BW, BW), BW)
+        return RB.at[mb, h, pl.ds(k % 2 * HB, HB), blk]
+
+    def out_remote(mb, q, k):
+        return pltpu.make_async_remote_copy(
+            src_ref=out_src(mb, q, k), dst_ref=out_dst(mb, k),
+            send_sem=o_send.at[mb, q, k], recv_sem=o_recv.at[mb, t, k],
+            device_id=((flip, s)[mb], q), device_id_type=MESH,
+        )
+
+    def out_start(mb, k):
+        for q in range(NT):
+            if mb == 0:
+                out_remote(mb, q, k).start()
+            else:
+                @pl.when(t != q)
+                def _():
+                    out_remote(mb, q, k).start()
+
+                @pl.when(t == q)
+                def _():
+                    pltpu.make_async_copy(out_src(mb, q, k), out_dst(mb, k), o_recv.at[mb, q, k]).start()
+
+    def out_sent(mb, k):
+        for q in range(NT):
+            if mb == 0:
+                out_remote(mb, q, k).wait_send()
+            else:
+                @pl.when(t != q)
+                def _():
+                    out_remote(mb, q, k).wait_send()
+
+    def sum_area(k):
+        return pl.ds(k % 2 * HB, HB), pl.ds(k // 2 * 2 * BW, 2 * BW)
+
+    def final_dst(mb, k):
+        return (od_hbm, ou_hbm)[mb].at[sum_area(k)]
+
+    def final_remote(mb, k):
+        return pltpu.make_async_remote_copy(
+            src_ref=U.at[(mb,) + sum_area(k)], dst_ref=final_dst(mb, k),
+            send_sem=f_send.at[mb, k], recv_sem=f_recv.at[mb, k],
+            device_id=((down_s, up_s)[mb], t), device_id_type=MESH,
+        )
+
+    def goes(mb):
+        return odd if mb == 0 else jnp.logical_not(up_self)
+
+    def relay_step(mb, k):
+        rows_k, cols_k = sum_area(k)
+        for q in range(NT):
+            blk = pl.ds((k // 2 * 2 + q % 2) * BW, BW)
+            landed = RB.at[mb, q // 2, rows_k, blk]
+            pltpu.make_async_copy(landed, landed, o_recv.at[mb, q, k]).wait()
+        total = RB[mb, 0, rows_k, cols_k].astype(f32) + RB[mb, 1, rows_k, cols_k].astype(f32)
+        first = (flip, s)[mb] == 0
+        U[(mb,) + sum_area(k)] = jnp.where(first, 0.0, total).astype(bf16)
+
+        @pl.when(goes(mb))
+        def _():
+            final_remote(mb, k).start()
+
+        @pl.when(jnp.logical_not(goes(mb)))
+        def _():
+            pltpu.make_async_copy(U.at[(mb,) + sum_area(k)], final_dst(mb, k), f_recv.at[mb, k]).start()
+
+    def forwards_sent():
+        for arr in range(2):
+            for q in range(NT):
+                for i in range(2):
+                    piece(U.at[arr], (X, C)[arr], 1, arr, q, i, (flip, q), t).wait_send()
+        for q in range(NT):
+            r_copy(1, q, (flip, q)).wait_send()
 
     w_copy.wait()
-    layer(0)
+    layer(0, None)
     v_copy(0).wait_send()
     gather_wait(1)
-    for q in range(NT):
-        for i in range(2):
-            out_remote(0, q, i).start()
-    layer(1)
-    for q in range(NT):
-        own = jnp.logical_and(up_self, t == q)
-        for i in range(2):
-            @pl.when(own)
-            def _():
-                out_local(q, i).start()
-
-            @pl.when(jnp.logical_not(own))
-            def _():
-                out_remote(1, q, i).start()
+    for k in range(CHUNKS):
+        out_start(0, k)
+    forwards_sent()
+    layer(1, relay_step)
+    out_start(1, 0)
+    out_start(1, 1)
 
     def fg_copy(q):
         return pltpu.make_async_remote_copy(
@@ -384,7 +445,14 @@
         dw_copy(j, slot).start()
         return carry
 
-    lax.fori_loop(0, tiles, dw_tile, 0)
+    for k in range(CHUNKS):
+        lax.fori_loop(k * tiles // CHUNKS, (k + 1) * tiles // CHUNKS, dw_tile, 0)
+        if k < 2:
+            relay_step(0, k + 2)
+        if k + 2 < CHUNKS:
+            out_sent(1, k)
+            out_start(1, k + 2)
+        relay_step(1, k)
     for j in (tiles - 2, tiles - 1):
         dw_copy(j, j % 2).wait()
 
@@ -399,28 +467,23 @@
             r_copy(0, q, (s, q)).wait_send()
             fg_copy(q).wait_send()
 
-        for arr in range(2):
-            for i in range(2):
-                piece(U.at[arr], (X, C)[arr], 1, arr, q, i, (flip, q), t).wait_send()
-        r_copy(1, q, (flip, q)).wait_send()
         pltpu.make_async_copy(FG, fg_hbm.at[q], fg_recv.at[q]).wait()
-        own = jnp.logical_and(up_self, t == q)
-        for i in range(2):
-            out_remote(0, q, i).wait_send()
-
-            @pl.when(jnp.logical_not(own))
-            def _():
-                out_remote(1, q, i).wait_send()
+    for k in range(CHUNKS):
+        out_sent(0, k)
+        if k >= CHUNKS - 2:
+            out_sent(1, k)
     v_copy(1).wait_send()
     for mb in range(2):
         pm_copy(mb).wait_send()
         for i in range(2):
             gv_copy(mb, i).wait_send()
-    for mb, dst in enumerate((od_hbm, ou_hbm)):
-        for q in range(NT):
-            for i in range(2):
-                landed = dst.at[q // 2, :, pl.ds((2 * i + q % 2) * BW, BW)]
-                pltpu.make_async_copy(landed, landed, o_recv.at[mb, q, i]).wait()
+    for mb in range(2):
+        for k in range(CHUNKS):
+            @pl.when(goes(mb))
+            def _():
+                final_remote(mb, k).wait_send()
+
+            pltpu.make_async_copy(final_dst(mb, k), final_dst(mb, k), f_recv.at[mb, k]).wait()
 
 
 def per_device(sections, weights, filters, down_input, down_cot, up_input, up_cot):
@@ -440,8 +503,8 @@
         out_shape=(
             jax.ShapeDtypeStruct((BW, D), bf16),
             jax.ShapeDtypeStruct((NT, n_groups, K), f32),
-            jax.ShapeDtypeStruct((2, TB, D), bf16),
-            jax.ShapeDtypeStruct((2, TB, D), bf16),
+            jax.ShapeDtypeStruct((TB, D), bf16),
+            jax.ShapeDtypeStruct((TB, D), bf16),
         ),
         in_specs=[hbm, pl.BlockSpec(memory_space=pltpu.VMEM), hbm, hbm, hbm, hbm],
         out_specs=(hbm, hbm, hbm, hbm),
@@ -463,12 +526,13 @@
             pltpu.VMEM((TOK, CW), bf16),
             pltpu.VMEM((2, 2, TOK, 128), f32),
             pltpu.VMEM((2, TOK, CW), bf16),
+            pltpu.VMEM((2, 2, TB, D), bf16),
             pltpu.VMEM((n_groups, K), f32),
             pltpu.VMEM((2, BW, DN), bf16),
             dma((2, 2, NT, 2)), dma((2, 2, NT, 2)), dma((2, NT)), dma((2, NT)),
             dma((2,)), dma((2,)), dma((2,)), dma((2,)),
             dma((2, 2)), dma((2, 2)), dma((2,)), dma((2,)),
-            dma((2, NT, 2)), dma((2, NT, 2)), dma((NT,)), dma((NT,)),
+            dma((2, NT, 4)), dma((2, NT, 4)), dma((2, 4)), dma((2, 4)), dma((NT,)), dma((NT,)),
             dma, dma, dma((2,)),
         ],
         compiler_params=pltpu.CompilerParams(
@@ -476,14 +540,9 @@
         ),
         name="relay_backward",
     )(w, taps, down_input[0], down_cot[0], up_input[0], up_cot[0])
-    s = lax.axis_index("section")
-    down = od[0].astype(f32) + od[1].astype(f32)
-    up = ou[0].astype(f32) + ou[1].astype(f32)
-    down = jnp.where(s == sections - 1, 0.0, down).astype(bf16)
-    up = jnp.where(s == 0, 0.0, up).astype(bf16)
     fg = fg.reshape(2, 2, 2, groups // NT, K)
     fg = jnp.transpose(fg[0] + fg[1], (1, 0, 2, 3)).reshape(groups, K)
-    return dw[None], fg[None], down[None], up[None]
+    return dw[None], fg[None], od[None], ou[None]
 
 
 def solution(mesh):

time: 224 us -> 195 us (0.87)
  the two profiles are of different devices: /device:TPU:91 before, /device:TPU:34 now
where the time goes in v2:
time: 195 us; the launch traced here: 194 us
  Pallas kernels  182 us (93%)
  local copies, waits for them, and re-layouts  10.6 us (5%)
    pallas_call x1, Pallas kernels, per_device(): pl.pallas_call(functools.partial(kernel, sections), out_shape=(jax.ShapeD...  182 us
    unnamed x7, local copies, waits for them, and re-layouts  9.98 us

profile of v2, /device:TPU:34, one launch (start us, length us, event | category | flops | bytes accessed | tf_op | source)
XLA Modules:
  0.0 194.1 jit_solution(3507121321181688753)
XLA Ops:
  0.6 182.1 %relay_backward.1 = (bf16[1024,4096]{1,0:T(8,128)(2,1)}, f32[4,16,128]{2,1,0:T(8,128)}, bf16[128,4096]{1,0:T(8,128)(2,1)}, bf16[128,4096]{1,0:T(8,128)(2,1)}) custom-call(bf16[1024,4096]{1,0:T(8,128)(2,1)} %bitcast.14, f32[32,128]{1,0:T(8,128)} %bitcast.22, bf16[128,4096]{1,0:T(8,128)(2,1)} %bitcast.16, bf16[128,4096]{1,0:T(8,128)(2,1)} %bitcast.17, ...), custom_call_target="tpu_custom_call" | custom-call | tf_op jit(solution)/shard_map/relay_backward/pallas_call | solution.py:501
  182.8 0.7 add_bitcast_fusion
  183.5 0.6 copy.10
  184.1 0.0 copy-start.1
  184.1 0.0 copy-start
  184.1 8.0 %copy.14 = bf16[1,1024,4096]{2,1,0:T(8,128)(2,1)} copy(bf16[1,1024,4096]{2,1,0:T(8,128)(2,1)} %bitcast.15) | data formatting | bytes 16777216
  192.1 0.0 copy-done.1
  192.1 1.0 copy.15
  193.1 0.0 copy-done
  193.1 1.0 copy.16
Async XLA Ops:
  184.1 8.0 %copy-start.1 = (bf16[128,4096]{1,0:T(8,128)(2,1)S(1)}, bf16[128,4096]{1,0:T(8,128)(2,1)}, u32[]{:S(2)}) copy-start(bf16[128,4096]{1,0:T(8,128)(2,1)} %get-tuple-element.10) | copy-start | bytes 3145732
  184.1 9.0 %copy-start = (bf16[128,4096]{1,0:T(8,128)(2,1)S(1)}, bf16[128,4096]{1,0:T(8,128)(2,1)}, u32[]{:S(2)}) copy-start(bf16[128,4096]{1,0:T(8,128)(2,1)} %get-tuple-element.11) | copy-start | bytes 3145732

commit v3 on v2

--- a/solution.py
+++ b/solution.py
@@ -26,7 +26,7 @@
     sections,
     w_hbm, f_ref, xd_hbm, cd_hbm, xu_hbm, cu_hbm,
     dw_hbm, fg_hbm, od_hbm, ou_hbm,
-    W, X, C, R, OWN, U, RS, T, TC, NBT, GV, VS, V, VR, G, PM, OS, RB, FG, DW,
+    W, X, C, R, OWN, U, RS, T, TC, NBT, GV, VS, V, VR, G, PM, OS, RB, PAIRS, FG, DW,
     g_send, g_recv, r_send, r_recv, u_send, u_recv, v_send, v_recv,
     gv_send, gv_recv, pm_send, pm_recv, o_send, o_recv, f_send, f_recv, fg_send, fg_recv,
     w_sem, own_sem, dw_sem,
@@ -97,7 +97,8 @@
             g_recv.at[mb, arr, q, i],
         )
 
-    for arr, (src, dst) in enumerate(((xd_hbm, X), (cd_hbm, C))):
+    def gather_start(arr):
+        src, dst = ((xd_hbm, X), (cd_hbm, C))[arr]
         for q in range(NT):
             @pl.when(t != q)
             def _():
@@ -116,8 +117,8 @@
             device_id=(relay, t), device_id_type=MESH,
         )
 
-    for arr in range(2):
-        relay_copy(arr).start()
+    gather_start(0)
+    relay_copy(0).start()
 
     def inverse_rms(ref):
         def step(j, acc):
@@ -160,17 +161,18 @@
         return carry
 
     lax.fori_loop(0, n_groups, build, 0)
-    FG[...] = jnp.zeros_like(FG)
-
-    def gather_wait(mb):
-        for arr, dst in enumerate((X, C)):
-            for q in range(NT):
-                for i in range(2):
-                    pltpu.make_async_copy(
-                        dst.at[mb, pl.ds(q * TB, TB), pl.ds(i * BW, BW)],
-                        dst.at[mb, pl.ds(q * TB, TB), pl.ds(i * BW, BW)],
-                        g_recv.at[mb, arr, q, i],
-                    ).wait()
+    relay_copy(0).wait_send()
+    gather_start(1)
+    relay_copy(1).start()
+
+    def gather_wait(mb, arr):
+        dst = (X, C)[arr]
+        for q in range(NT):
+            for i in range(2):
+                landed = dst.at[mb, pl.ds(q * TB, TB), pl.ds(i * BW, BW)]
+                pltpu.make_async_copy(landed, landed, g_recv.at[mb, arr, q, i]).wait()
+
+    def r_wait(mb):
         for q in range(NT):
             def wait_r():
                 pltpu.make_async_copy(RS.at[mb], R.at[mb, pl.ds(q * TB, TB), :], r_recv.at[mb, q]).wait()
@@ -179,16 +181,15 @@
             else:
                 wait_r()
 
-    gather_wait(0)
-
-    for arr in range(2):
-        relay_copy(arr).wait_recv()
+    def forward(arr):
         for q in range(NT):
             for i in range(2):
                 piece(U.at[arr], (X, C)[arr], 1, arr, q, i, (flip, q), t).start()
-    RS[1] = inverse_rms(U.at[0])
-    for q in range(NT):
-        r_copy(1, q, (flip, q)).start()
+
+    def forward_sent(arr):
+        for q in range(NT):
+            for i in range(2):
+                piece(U.at[arr], (X, C)[arr], 1, arr, q, i, (flip, q), t).wait_send()
 
     def cols(j, width=gw):
         return pl.ds(pl.multiple_of(j * width, width), width)
@@ -225,23 +226,21 @@
 
     VN = min(512, BW)
     RN = min(256, BW)
-
-    def layer(mb, between):
-        def prep(gi, carry):
-            n = X[mb, :, cols(gi)].astype(f32) * R[mb]
-            gm = (C[mb, :, cols(gi)].astype(f32) * n).astype(bf16)
-            X[mb, :, cols(gi)] = n.astype(bf16)
-            w = windows(jnp.concatenate([gm, zero_block], axis=0))
-            gv = matmul(T[gi], w).astype(bf16)
-            for i in range(NT):
-                GV[mb * TOK + i * TB : mb * TOK + (i + 1) * TB, cols(natural(gi))] = gv[:, i * gw : (i + 1) * gw]
-            return carry
-
-        lax.fori_loop(0, n_groups, prep, 0)
-        for i in range(2):
-            gv_copy(mb, i).start()
-
-        own_cols = pl.ds(pl.multiple_of(h * BW, BW), BW)
+    UN = 2
+    wide = min(512, BW)
+    own_cols = pl.ds(pl.multiple_of(h * BW, BW), BW)
+
+    def blocks(x):
+        return [x[i * TB : (i + 1) * TB] for i in range(NT)]
+
+    def values(mb):
+        def norm(gi, carry):
+            at = cols(gi, 2 * gw)
+            scale = jnp.concatenate([R[mb], R[mb]], axis=1)
+            X[mb, :, at] = (X[mb, :, at].astype(f32) * scale).astype(bf16)
+            return carry
+
+        lax.fori_loop(0, n_groups // 2, norm, 0)
 
         def sib_values(j, carry):
             src = (j // (BW // VN) * 2 + (1 - c)) * (BW // VN) + lax.rem(j, BW // VN)
@@ -263,35 +262,46 @@
             return carry
 
         lax.fori_loop(0, per_block, turn, 0)
+
+    def mixed_grad(mb, gi):
+        gm = C[mb, :, cols(gi)].astype(f32) * X[mb, :, cols(gi)].astype(f32)
+        return windows(jnp.concatenate([gm.astype(bf16), zero_block], axis=0))
+
+    def grads(mb):
+        def grad(j, carry):
+            gs = [j * UN + u for u in range(UN)]
+            ws = [mixed_grad(mb, gi) for gi in gs]
+            gvs = [matmul(T[gi], w).astype(bf16) for gi, w in zip(gs, ws)]
+            for gi, gv in zip(gs, gvs):
+                for i in range(NT):
+                    GV[mb * TOK + i * TB : mb * TOK + (i + 1) * TB, cols(natural(gi))] = gv[:, i * gw : (i + 1) * gw]
+            return carry
+
+        lax.fori_loop(0, n_groups // UN, grad, 0)
+        for i in range(2):
+            gv_copy(mb, i).start()
+
+    def convolve(mb):
         v_copy(mb).wait_recv()
 
-        def mix(gi, carry):
-            v = (V[:, cols(gi)].astype(f32) + VR[mb, :, cols(gi)].astype(f32)).astype(bf16)
-            cot = C[mb, :, cols(gi)].astype(f32)
-            gm = (cot * X[mb, :, cols(gi)].astype(f32)).astype(bf16)
-            conv = matmul(TC[gi], windows(jnp.concatenate([zero_block, v], axis=0)))
-            for i in range(NT):
-                part = slice(i * TB, (i + 1) * TB)
-                G[part, cols(gi)] = (cot[part] * conv[:, i * gw : (i + 1) * gw]).astype(bf16)
-            v_side = jnp.concatenate([v[i * TB : (i + 1) * TB] for i in range(NT)], axis=1)
-            x = contract_last(v_side, windows(jnp.concatenate([gm, zero_block], axis=0)))
-            n = TB
-            while n > 1:
-                half = n // 2
-                x = x[:half] + pltpu.roll(x[half:n], 2 * TB - half, 1)
-                n = half
-            FG[pl.ds(gi, 1), :] = FG[pl.ds(gi, 1), :] + x[:, :TB]
-            return carry
-
-        lax.fori_loop(0, n_groups, mix, 0)
-
-        if between is not None:
-            between(0, 0)
+        def mix(j, carry):
+            gs = [j * UN + u for u in range(UN)]
+            vs = [(V[:, cols(gi)].astype(f32) + VR[mb, :, cols(gi)].astype(f32)).astype(bf16) for gi in gs]
+            cots = [C[mb, :, cols(gi)].astype(f32) for gi in gs]
+            convs = [matmul(TC[gi], windows(jnp.concatenate([zero_block, v], axis=0))) for gi, v in zip(gs, vs)]
+            for gi, v, cot, conv in zip(gs, vs, cots, convs):
+                VR[mb, :, cols(gi)] = v
+                conv = jnp.concatenate([conv[:, i * gw : (i + 1) * gw] for i in range(NT)], axis=0)
+                G[:, cols(gi)] = (cot * conv).astype(bf16)
+            return carry
+
+        lax.fori_loop(0, n_groups // UN, mix, 0)
+
+    def back(mb):
         for i in range(2):
             blk = pl.ds(pl.multiple_of((2 * i + 1 - c) * BW, BW), BW)
-            pltpu.make_async_copy(
-                GV.at[pl.ds(mb * TOK, TOK), blk], GV.at[pl.ds(mb * TOK, TOK), blk], gv_recv.at[mb, i]
-            ).wait()
+            landed = GV.at[pl.ds(mb * TOK, TOK), blk]
+            pltpu.make_async_copy(landed, landed, gv_recv.at[mb, i]).wait()
 
         def returned(j, carry):
             res = contract_last(GV[mb * TOK : (mb + 1) * TOK, :], W[pl.ds(pl.multiple_of(j * RN, RN), RN), :])
@@ -300,26 +310,54 @@
             return carry
 
         lax.fori_loop(0, BW // RN, returned, 0)
-        if between is not None:
-            between(0, 1)
-
-        def moment(gi, acc):
-            return acc + G[:, cols(gi)].astype(f32) * X[mb, :, cols(gi)].astype(f32)
-
-        PM[mb, 0] = lax.fori_loop(0, n_groups, moment, jnp.zeros((TOK, gw), f32))
+
+    def finish(mb):
+        def moment(j, acc):
+            at = cols(j, wide)
+            x = G[:, at].astype(f32) * X[mb, :, at].astype(f32)
+            return acc + sum(x[:, i * gw : (i + 1) * gw] for i in range(wide // gw))
+
+        PM[mb, 0] = lax.fori_loop(0, CW // wide, moment, jnp.zeros((TOK, gw), f32))
         pm_copy(mb).start()
         pm_copy(mb).wait_recv()
         mean = jnp.sum(PM[mb, 0] + PM[mb, 1], axis=1, keepdims=True) / D
         PM[mb, 1] = jnp.broadcast_to(mean, (TOK, gw))
         keep = jnp.where(h == 0, 1.0, 0.0).astype(f32)
 
-        def final(gi, carry):
-            n = X[mb, :, cols(gi)].astype(f32)
-            grad = R[mb] * (G[:, cols(gi)].astype(f32) - n * PM[mb, 1])
-            OS[mb, :, cols(gi)] = (grad + keep * C[mb, :, cols(gi)].astype(f32)).astype(bf16)
-            return carry
-
-        lax.fori_loop(0, n_groups, final, 0)
+        def final(j, carry):
+            at = cols(j, 2 * gw)
+            scale = jnp.concatenate([R[mb], R[mb]], axis=1)
+            pm = jnp.concatenate([PM[mb, 1], PM[mb, 1]], axis=1)
+            grad = scale * (G[:, at].astype(f32) - X[mb, :, at].astype(f32) * pm)
+            OS[mb, :, at] = (grad + keep * C[mb, :, at].astype(f32)).astype(bf16)
+            return carry
+
+        lax.fori_loop(0, n_groups // 2, final, 0)
+
+    def tap_pairs(mb):
+        def pairs(j, carry):
+            gs = [j * UN + u for u in range(UN)]
+            ws = [mixed_grad(mb, gi) for gi in gs]
+            vs = [jnp.concatenate(blocks(VR[mb, :, cols(gi)]), axis=1) for gi in gs]
+            ps = [contract_last(v, w) for v, w in zip(vs, ws)]
+            for gi, p in zip(gs, ps):
+                PAIRS[gi] = p if mb == 0 else PAIRS[gi] + p
+            return carry
+
+        lax.fori_loop(0, n_groups // UN, pairs, 0)
+
+    def tap_sums():
+        n = TB
+        while n > 8:
+            half = n // 2
+            for gi in range(n_groups):
+                PAIRS[gi, :half] = PAIRS[gi, :half] + pltpu.roll(PAIRS[gi, half:n], 2 * TB - half, 1)
+            n = half
+        for gi in range(n_groups):
+            x = PAIRS[gi, :8]
+            for half in (4, 2, 1):
+                x = x[:half] + pltpu.roll(x[half:], 2 * TB - half, 1)
+            FG[gi : gi + 1, :] = x[:, :TB]
 
     HB = TB // 2
     CHUNKS = 4
@@ -394,24 +432,44 @@
         def _():
             pltpu.make_async_copy(U.at[(mb,) + sum_area(k)], final_dst(mb, k), f_recv.at[mb, k]).start()
 
-    def forwards_sent():
-        for arr in range(2):
-            for q in range(NT):
-                for i in range(2):
-                    piece(U.at[arr], (X, C)[arr], 1, arr, q, i, (flip, q), t).wait_send()
-        for q in range(NT):
-            r_copy(1, q, (flip, q)).wait_send()
-
+    relay_copy(0).wait_recv()
+    forward(0)
+    RS[1] = inverse_rms(U.at[0])
+    for q in range(NT):
+        r_copy(1, q, (flip, q)).start()
+    r_wait(0)
+    gather_wait(0, 0)
     w_copy.wait()
-    layer(0, None)
+    values(0)
+    relay_copy(1).wait_recv()
+    forward_sent(0)
+    forward(1)
+    gather_wait(0, 1)
+    grads(0)
+    convolve(0)
+    back(0)
+    finish(0)
+    out_start(0, 0)
     v_copy(0).wait_send()
-    gather_wait(1)
-    for k in range(CHUNKS):
+    r_wait(1)
+    gather_wait(1, 0)
+    values(1)
+    gather_wait(1, 1)
+    for k in range(1, CHUNKS):
         out_start(0, k)
-    forwards_sent()
-    layer(1, relay_step)
+    forward_sent(1)
+    grads(1)
+    convolve(1)
+    back(1)
+    relay_step(0, 0)
+    finish(1)
     out_start(1, 0)
     out_start(1, 1)
+    relay_step(0, 1)
+    tap_pairs(0)
+    relay_step(0, 2)
+    tap_pairs(1)
+    tap_sums()
 
     def fg_copy(q):
         return pltpu.make_async_remote_copy(
@@ -447,8 +505,8 @@
 
     for k in range(CHUNKS):
         lax.fori_loop(k * tiles // CHUNKS, (k + 1) * tiles // CHUNKS, dw_tile, 0)
-        if k < 2:
-            relay_step(0, k + 2)
+        if k == 0:
+            relay_step(0, 3)
         if k + 2 < CHUNKS:
             out_sent(1, k)
             out_start(1, k + 2)
@@ -456,9 +514,10 @@
     for j in (tiles - 2, tiles - 1):
         dw_copy(j, j % 2).wait()
 
-    for arr in range(2):
-        relay_copy(arr).wait_send()
+    relay_copy(1).wait_send()
     for q in range(NT):
+        r_copy(1, q, (flip, q)).wait_send()
+
         @pl.when(t != q)
         def _():
             for arr, (src, dst) in enumerate(((xd_hbm, X), (cd_hbm, C))):
@@ -484,6 +543,24 @@
                 final_remote(mb, k).wait_send()
 
             pltpu.make_async_copy(final_dst(mb, k), final_dst(mb, k), f_recv.at[mb, k]).wait()
+
+
+PARTS = 16
+
+
+def settle(dw_in, od_in, ou_in, dw_out, od_out, ou_out, dw_buf, od_buf, ou_buf, load_sems, save_sems):
+    rows = dw_in.shape[0] // PARTS
+    pieces = [(dw_in.at[pl.ds(p * rows, rows)], dw_buf.at[pl.ds(p * rows, rows)], dw_out.at[pl.ds(p * rows, rows)]) for p in range(PARTS)]
+    pieces += [(od_in, od_buf, od_out), (ou_in, ou_buf, ou_out)]
+    loads = [pltpu.make_async_copy(src, buf, load_sems.at[p]) for p, (src, buf, _) in enumerate(pieces)]
+    saves = [pltpu.make_async_copy(buf, dst, save_sems.at[p]) for p, (_, buf, dst) in enumerate(pieces)]
+    for load in loads:
+        load.start()
+    for load, save in zip(loads, saves):
+        load.wait()
+        save.start()
+    for save in saves:
+        save.wait()
 
 
 def per_device(sections, weights, filters, down_input, down_cot, up_input, up_cot):
@@ -527,6 +604,7 @@
             pltpu.VMEM((2, 2, TOK, 128), f32),
             pltpu.VMEM((2, TOK, CW), bf16),
             pltpu.VMEM((2, 2, TB, D), bf16),
+            pltpu.VMEM((n_groups, TB, 2 * TB), f32),
             pltpu.VMEM((n_groups, K), f32),
             pltpu.VMEM((2, BW, DN), bf16),
             dma((2, 2, NT, 2)), dma((2, 2, NT, 2)), dma((2, NT)), dma((2, NT)),
@@ -540,6 +618,15 @@
         ),
         name="relay_backward",
     )(w, taps, down_input[0], down_cot[0], up_input[0], up_cot[0])
+    dw, od, ou = pl.pallas_call(
+        settle,
+        out_shape=tuple(jax.ShapeDtypeStruct(x.shape, bf16) for x in (dw, od, ou)),
+        in_specs=[hbm, hbm, hbm],
+        out_specs=(hbm, hbm, hbm),
+        scratch_shapes=[pltpu.VMEM(x.shape, bf16) for x in (dw, od, ou)] + [dma((PARTS + 2,)), dma((PARTS + 2,))],
+        compiler_params=pltpu.CompilerParams(vmem_limit_bytes=60 * 1024 * 1024),
+        name="settle",
+    )(dw, od, ou)
     fg = fg.reshape(2, 2, 2, groups // NT, K)
     fg = jnp.transpose(fg[0] + fg[1], (1, 0, 2, 3)).reshape(groups, K)
     return dw[None], fg[None], od[None], ou[None]

time: 195 us -> 175 us (0.90)
  local copies, waits for them, and re-layouts: 10.6 us -> 0.61 us
  Pallas kernels: 182 us -> 173 us
    pallas_call x1, Pallas kernels: 182 us -> 165 us  [per_device(): pl.pallas_call(functools.partial(kernel, sections), out_shape=(jax.ShapeD...]
    unnamed x7 -> x2, local copies, waits for them, and re-layouts: 9.98 us -> 0.01 us
    pallas_call x0 -> x1, Pallas kernels: none -> 8.21 us  [per_device(): pl.pallas_call(settle, out_shape=tuple((jax.ShapeDtypeStruct(x.shape, bf1...]
where the time goes in v3:
time: 175 us; the launch traced here: 174 us
  Pallas kernels  173 us (99%)
    pallas_call x1, Pallas kernels, per_device(): pl.pallas_call(functools.partial(kernel, sections), out_shape=(jax.ShapeD...  165 us
    pallas_call x1, Pallas kernels, per_device(): pl.pallas_call(settle, out_shape=tuple((jax.ShapeDtypeStruct(x.shape, bf1...  8.21 us

profile of v3, /device:TPU:34, one launch (start us, length us, event | category | flops | bytes accessed | tf_op | source)
XLA Modules:
  0.0 174.5 jit_solution(13345908137575905774)
XLA Ops:
  0.6 165.0 %relay_backward.1 = (bf16[1024,4096]{1,0:T(8,128)(2,1)}, f32[4,16,128]{2,1,0:T(8,128)}, bf16[128,4096]{1,0:T(8,128)(2,1)}, bf16[128,4096]{1,0:T(8,128)(2,1)}) custom-call(bf16[1024,4096]{1,0:T(8,128)(2,1)} %bitcast.14, f32[32,128]{1,0:T(8,128)} %bitcast.19, bf16[128,4096]{1,0:T(8,128)(2,1)} %bitcast.15, bf16[128,4096]{1,0:T(8,128)(2,1)} %bitcast.16, ...), custom_call_target="tpu_custom_call" | custom-call | tf_op jit(solution)/shard_map/relay_backward/pallas_call | solution.py:578
  165.6 0.0 copy-start
  165.6 8.2 %settle.1 = (bf16[1024,4096]{1,0:T(8,128)(2,1)}, bf16[128,4096]{1,0:T(8,128)(2,1)}, bf16[128,4096]{1,0:T(8,128)(2,1)}) custom-call(bf16[1024,4096]{1,0:T(8,128)(2,1)} %get-tuple-element.11.dw_in, bf16[128,4096]{1,0:T(8,128)(2,1)} %get-tuple-element.12.od_in, bf16[128,4096]{1,0:T(8,128)(2,1)} %get-tuple-element.13.ou_in), custom_call_target="tpu_custom_call" | custom-call | tf_op jit(solution)/shard_map/settle/pallas_call | solution.py:621
  173.8 0.0 copy-done
  173.8 0.6 copy.10
  (1 shorter events, 0.0 us)
Async XLA Ops:
  165.6 8.2 %copy-start = (f32[4,16,128]{2,1,0:T(8,128)S(1)}, f32[4,16,128]{2,1,0:T(8,128)}, u32[]{:S(2)}) copy-start(f32[4,16,128]{2,1,0:T(8,128)} %get-tuple-element.15) | copy-start | bytes 98308

commit v4 on v3

--- a/solution.py
+++ b/solution.py
@@ -117,8 +117,9 @@
             device_id=(relay, t), device_id_type=MESH,
         )
 
+    relay_copy(0).start()
     gather_start(0)
-    relay_copy(0).start()
+    gather_start(1)
 
     def inverse_rms(ref):
         def step(j, acc):
@@ -162,7 +163,6 @@
 
     lax.fori_loop(0, n_groups, build, 0)
     relay_copy(0).wait_send()
-    gather_start(1)
     relay_copy(1).start()
 
     def gather_wait(mb, arr):
@@ -545,7 +545,7 @@
             pltpu.make_async_copy(final_dst(mb, k), final_dst(mb, k), f_recv.at[mb, k]).wait()
 
 
-PARTS = 16
+PARTS = 4
 
 
 def settle(dw_in, od_in, ou_in, dw_out, od_out, ou_out, dw_buf, od_buf, ou_buf, load_sems, save_sems):

time: 175 us -> 174 us (level)
  no operation moved by 1% of the time
where the time goes in v4:
time: 174 us
  Pallas kernels  173 us (99%)
    pallas_call x1, Pallas kernels, per_device(): pl.pallas_call(functools.partial(kernel, sections), out_shape=(jax.ShapeD...  165 us
    pallas_call x1, Pallas kernels, per_device(): pl.pallas_call(settle, out_shape=tuple((jax.ShapeDtypeStruct(x.shape, bf1...  7.67 us

profile of v4, /device:TPU:34, one launch (start us, length us, event | category | flops | bytes accessed | tf_op | source)
XLA Modules:
  0.0 173.9 jit_solution(5401390907259799496)
XLA Ops:
  0.6 165.0 %relay_backward.1 = (bf16[1024,4096]{1,0:T(8,128)(2,1)}, f32[4,16,128]{2,1,0:T(8,128)}, bf16[128,4096]{1,0:T(8,128)(2,1)}, bf16[128,4096]{1,0:T(8,128)(2,1)}) custom-call(bf16[1024,4096]{1,0:T(8,128)(2,1)} %bitcast.14, f32[32,128]{1,0:T(8,128)} %bitcast.19, bf16[128,4096]{1,0:T(8,128)(2,1)} %bitcast.15, bf16[128,4096]{1,0:T(8,128)(2,1)} %bitcast.16, ...), custom_call_target="tpu_custom_call" | custom-call | tf_op jit(solution)/shard_map/relay_backward/pallas_call | solution.py:578
  165.6 0.0 copy-start
  165.6 7.7 %settle.1 = (bf16[1024,4096]{1,0:T(8,128)(2,1)}, bf16[128,4096]{1,0:T(8,128)(2,1)}, bf16[128,4096]{1,0:T(8,128)(2,1)}) custom-call(bf16[1024,4096]{1,0:T(8,128)(2,1)} %get-tuple-element.11.dw_in, bf16[128,4096]{1,0:T(8,128)(2,1)} %get-tuple-element.12.od_in, bf16[128,4096]{1,0:T(8,128)(2,1)} %get-tuple-element.13.ou_in), custom_call_target="tpu_custom_call" | custom-call | tf_op jit(solution)/shard_map/settle/pallas_call | solution.py:621
  173.3 0.0 copy-done
  173.3 0.6 copy.10
  (1 shorter events, 0.0 us)
Async XLA Ops:
  165.6 7.7 %copy-start = (f32[4,16,128]{2,1,0:T(8,128)S(1)}, f32[4,16,128]{2,1,0:T(8,128)}, u32[]{:S(2)}) copy-start(f32[4,16,128]{2,1,0:T(8,128)} %get-tuple-element.15) | copy-start | bytes 98308
